TPU v7x, 32 devices: a whole 2x2x4 slice. The times are simulated.
32 devices in a mesh: rows: 4 (over x, core), cols: 8 (over z, y).
Axes of the slice: x: 2, y: 2, z: 4, core: 2. Of those that a mesh axis runs over, the one named last changes fastest.
Arguments:
- image: bfloat16 [48, 64, 2048], P(None, 'rows', 'cols'), may hold values from -6 to 6
- perturb: float32 [48, 64, 2048], P(None, 'rows', 'cols'), may hold values from -0.5 to 0.5
- target: bfloat16 [48, 32, 1024], P(None, 'rows', 'cols'), may hold values from -6 to 6
- kernel_one: float32 [48, 48, 3, 3], replicated, may hold values from -0.3125 to 0.3125
- kernel_two: float32 [48, 48, 3, 3], replicated, may hold values from -0.3125 to 0.3125
- moment_one: float32 [48, 48, 3, 3], replicated, may hold values from -6 to 6
- moment_two: float32 [48, 48, 3, 3], replicated, may hold values from -6 to 6
Outputs:
- new_perturb: float32 [48, 64, 2048], P(None, 'rows', 'cols')
- prediction: bfloat16 [48, 32, 1024], P(None, 'rows', 'cols')
- new_kernel_one: float32 [48, 48, 3, 3], replicated
- new_kernel_two: float32 [48, 48, 3, 3], replicated
- new_moment_one: float32 [48, 48, 3, 3], replicated
- new_moment_two: float32 [48, 48, 3, 3], replicated
All inputs are finite; a program needn't handle non-finite values.
Results may differ from a plain program's by a relative error of at most 0.0085.
Values may be sent and summed in bfloat16 or wider, within the bound.
A program may use at most 128 MiB of HBM per device.

v0:
```python
import jax
import jax.numpy as jnp
from jax import lax
from jax.sharding import PartitionSpec as P

REPLAYS = 3
step_size = 0.5
clip_bound = 0.5
momentum_rate = 0.9
learn_rate = 0.005
mean_epsilon = 1e-06
numbers = ("NCHW", "OIHW", "NCHW")


def with_halo(block, sides, width):
    for axis, dim in sides:
        count = lax.axis_size(axis)
        forward = [(i, i + 1) for i in range(count - 1)]
        backward = [(target, source) for source, target in forward]
        low = lax.ppermute(
            lax.slice_in_dim(block, block.shape[dim] - width, None, axis=dim), axis, forward
        )
        high = lax.ppermute(lax.slice_in_dim(block, 0, width, axis=dim), axis, backward)
        block = jnp.concatenate([low, block, high], axis=dim)
    return block


def shifted(block, axis, distance):
    devices = range(lax.axis_size(axis))
    route = [(i - distance, i) for i in devices if i - distance in devices]
    return lax.ppermute(block, axis, route)


def plain_conv(source, kernel, stride, dilation):
    return lax.conv_general_dilated(
        source[None],
        kernel,
        (stride, stride),
        "VALID",
        rhs_dilation=(dilation, dilation),
        dimension_numbers=numbers,
        preferred_element_type=jnp.float32,
    )[0]


def kernel_grad(source, grad_out, stride, dilation):
    summed = lax.conv_general_dilated(
        source[None],
        grad_out[None],
        (dilation, dilation),
        "VALID",
        rhs_dilation=(stride, stride),
        dimension_numbers=("CNHW", "IOHW", "NCHW"),
        preferred_element_type=jnp.float32,
    )
    return jnp.transpose(summed, (1, 0, 2, 3))


def flipped(kernel):
    return jnp.transpose(kernel, (1, 0, 2, 3))[:, :, ::-1, ::-1]


def spread_grad(grad_out, kernel):
    return lax.conv_general_dilated(
        grad_out[None],
        flipped(kernel),
        (1, 1),
        ((2, 2), (2, 2)),
        lhs_dilation=(2, 2),
        dimension_numbers=numbers,
        preferred_element_type=jnp.float32,
    )[0]


def silu_slope(pre_value):
    sigmoid_value = jax.nn.sigmoid(pre_value)
    return sigmoid_value * (1.0 + pre_value * (1.0 - sigmoid_value))


def normed_update(kernel, moment, gradient, mean_square):
    moment = momentum_rate * moment + gradient / jnp.sqrt(mean_square + mean_epsilon)
    return (kernel - learn_rate * moment, moment)


def body(image, perturb, target, kernel_one, kernel_two, moment_one, moment_two):
    target_wide = target.astype(jnp.float32)
    learned = [kernel_one, moment_one, kernel_two, moment_two]
    fast_one = kernel_one.astype(jnp.bfloat16)
    fast_two = kernel_two.astype(jnp.bfloat16)
    predict = jnp.zeros(target.shape, jnp.float32)
    for replay in range(REPLAYS):
        attacked = (image.astype(jnp.float32) + perturb).astype(jnp.bfloat16)
        beside_all = with_halo(attacked, (("rows", 1), ("cols", 2)), 2)
        hidden_pre = plain_conv(beside_all, fast_one, 1, 2)
        hidden = jax.nn.silu(hidden_pre).astype(jnp.bfloat16)
        left_col = shifted(hidden[:, :, -1:], "cols", 1)
        widened = jnp.concatenate([left_col, hidden], axis=2)
        top_row = shifted(widened[:, -1:, :], "rows", 1)
        extended = jnp.concatenate([top_row, widened], axis=1)
        predict = plain_conv(extended, fast_two, 2, 1)
        residual = (predict - target_wide).astype(jnp.bfloat16)
        grad_two = kernel_grad(extended, residual, 2, 1)
        grad_two = lax.psum(grad_two, ("rows", "cols"))
        spread = spread_grad(residual, fast_two)
        from_below = shifted(spread[:, :1, :].astype(jnp.bfloat16), "rows", -1).astype(jnp.float32)
        widened_grad = spread[:, 1:, :].at[:, -1:, :].add(from_below)
        from_right = shifted(widened_grad[:, :, :1], "cols", -1)
        hidden_grad = widened_grad[:, :, 1:].at[:, :, -1:].add(from_right)
        pre_grad = (hidden_grad * silu_slope(hidden_pre)).astype(jnp.bfloat16)
        grad_rimmed = with_halo(pre_grad, (("rows", 1), ("cols", 2)), 2)
        input_grad = plain_conv(grad_rimmed, flipped(fast_one), 1, 2)
        grad_one = kernel_grad(beside_all, pre_grad, 1, 2)
        perturb = jnp.clip(perturb + step_size * jnp.tanh(input_grad), -clip_bound, clip_bound)
        grad_one = lax.psum(grad_one, ("rows", "cols"))
        new_one, new_moment_one = normed_update(
            learned[0], learned[1], grad_one, jnp.mean(grad_one * grad_one)
        )
        new_two, new_moment_two = normed_update(
            learned[2], learned[3], grad_two, jnp.mean(grad_two * grad_two)
        )
        learned = [new_one, new_moment_one, new_two, new_moment_two]
        fast_one = new_one.astype(jnp.bfloat16)
        fast_two = new_two.astype(jnp.bfloat16)
    return (perturb, predict.astype(jnp.bfloat16), learned[0], learned[2], learned[1], learned[3])


def solution(mesh):
    in_specs = (
        P(None, "rows", "cols"),
        P(None, "rows", "cols"),
        P(None, "rows", "cols"),
        P(),
        P(),
        P(),
        P(),
    )
    out_specs = (P(None, "rows", "cols"), P(None, "rows", "cols"), P(), P(), P(), P())
    return jax.shard_map(body, mesh=mesh, in_specs=in_specs, out_specs=out_specs, check_vma=False)
```

profile of v0, /device:TPU:8, one launch (start us, length us, event | category | flops | bytes accessed | tf_op | source)
XLA Modules:
  0.0 782.5 jit_solution(5333286303783374361)
XLA Ops:
  28.6 7.8 collective-permute-done.3
  80.5 5.1 scatter-add.20
  93.5 4.9 copy.320
  98.4 4.7 copy.329
  106.5 5.5 collective-permute-start.8
  113.3 5.5 fusion.109
  127.2 14.8 %fusion.22 = f32[48,48,3,3]{0,1,3,2:T(8,128)} fusion(bf16[1,48,20,260]{1,0,3,2:T(2,128)(2,1)} %copy.320, bf16[1,48,16,256]{1,2,3,0:T(8,128)(2,1)S(1)} %bitcast.267), kind=kOutput, calls=%fused_computation.48 | convolution fusion | flops 169869312 | bytes 975360 | tf_op jit(solution)/shard_map/transpose | solution.py:56
  158.1 113.7 %all-reduce.11.cloned.1.call-done = (f32[48,48,3,3]{0,1,3,2:T(8,128)}, f32[48,48,3,3]{0,1,3,2:T(8,128)}) async-done(((f32[48,48,3,3]{0,1,3,2:T(8,128)}, f32[48,48,3,3]{0,1,3,2:T(8,128)}), (f32[48,48,3,3]{0,1,3,2:T(8,128)}, f32[48,48,3,3]{0,1,3,2:T(8,128)})) %all-reduce.11.cloned.1.call-update) | async-done | bytes 165904 | tf_op jit(solution)/shard_map/psum | solution.py:114
  282.9 4.1 collective-permute-done.14
  329.9 5.1 scatter-add.24
  337.6 4.9 copy.348
  342.5 4.7 copy.355
  350.6 6.2 collective-permute-start.20
  358.1 5.5 fusion.107
  371.8 14.8 %fusion.20 = f32[48,48,3,3]{0,1,3,2:T(8,128)} fusion(bf16[1,48,20,260]{1,0,3,2:T(2,128)(2,1)} %copy.348, bf16[1,48,16,256]{1,2,3,0:T(8,128)(2,1)S(1)} %bitcast.268), kind=kOutput, calls=%fused_computation.46 | convolution fusion | flops 169869312 | bytes 975360 | tf_op jit(solution)/shard_map/transpose | solution.py:56
  403.4 112.0 %all-reduce.9.cloned.1.call-done = (f32[48,48,3,3]{0,1,3,2:T(8,128)}, f32[48,48,3,3]{0,1,3,2:T(8,128)}) async-done(((f32[48,48,3,3]{0,1,3,2:T(8,128)}, f32[48,48,3,3]{0,1,3,2:T(8,128)}), (f32[48,48,3,3]{0,1,3,2:T(8,128)}, f32[48,48,3,3]{0,1,3,2:T(8,128)})) %all-reduce.9.cloned.1.call-update) | async-done | bytes 165904 | tf_op jit(solution)/shard_map/psum | solution.py:114
  527.4 4.2 collective-permute-done.26
  574.5 4.9 copy.368
  582.9 4.7 copy.370
  589.0 5.1 scatter-add.26
  596.7 7.1 fusion.105
  605.0 4.8 collective-permute-start.32
  622.2 14.8 %fusion.18 = f32[48,48,3,3]{0,1,3,2:T(8,128)} fusion(bf16[1,48,20,260]{1,0,3,2:T(2,128)(2,1)} %copy.368, bf16[1,48,16,256]{1,2,3,0:T(8,128)(2,1)S(1)} %bitcast.269), kind=kOutput, calls=%fused_computation.44 | convolution fusion | flops 169869312 | bytes 975360 | tf_op jit(solution)/shard_map/transpose | solution.py:56
  650.2 117.2 %all-reduce.7.cloned.1.call-done = (f32[48,48,3,3]{0,1,3,2:T(8,128)}, f32[48,48,3,3]{0,1,3,2:T(8,128)}) async-done(((f32[48,48,3,3]{0,1,3,2:T(8,128)}, f32[48,48,3,3]{0,1,3,2:T(8,128)}), (f32[48,48,3,3]{0,1,3,2:T(8,128)}, f32[48,48,3,3]{0,1,3,2:T(8,128)})) %all-reduce.7.cloned.1.call-update) | async-done | bytes 165904 | tf_op jit(solution)/shard_map/psum | solution.py:114
  (396 shorter events, 280.0 us)
Async XLA Ops:
  7.2 264.7 %all-reduce.11.cloned.1.call-start = ((), (), s32[]{:S(2)}) async-start(), calls=%async_computation.2 | async-start | bytes 884736 | tf_op jit(solution)/shard_map/psum | solution.py:114
  23.0 13.4 %collective-permute-start.3 = (bf16[48,20,2]{2,0,1:T(8,128)(2,1)S(1)}, bf16[48,20,2]{2,0,1:T(8,128)(2,1)S(1)}, u32[]{:S(2)}, u32[]{:S(2)}) collective-permute-start(bf16[48,20,2]{2,0,1:T(8,128)(2,1)S(1)} %get-tuple-element.163), channel_id=1, source_target_pairs={{1,0},{2,1},{3,2},{4,3},{5,4},{6,5},{7,6},{9,8},{10,9},{11,10},{12... | collective-permute-start | bytes 11528 | tf_op jit(solution)/shard_map/ppermute | solution.py:23
  86.3 18.5 %collective-permute-start.7 = (f32[48,16,1]{0,1,2:T(8,128)S(1)}, f32[48,16,1]{0,1,2:T(8,128)S(1)}, u32[]{:S(2)}, u32[]{:S(2)}) collective-permute-start(f32[48,16,1]{0,1,2:T(8,128)S(1)} %slice.369), channel_id=1, source_target_pairs={{1,0},{2,1},{3,2},{4,3},{5,4},{6,5},{7,6},{9,8},{10,9},{11,10},{12... | collective-permute-start | bytes 9224 | tf_op jit(solution)/shard_map/ppermute | solution.py:31
  106.5 13.2 %collective-permute-start.8 = (bf16[48,2,256]{0,1,2:T(2,128)(2,1)S(1)}, bf16[48,2,256]{0,1,2:T(2,128)(2,1)S(1)}, u32[]{:S(2)}, u32[]{:S(2)}) collective-permute-start(bf16[48,2,256]{0,1,2:T(2,128)(2,1)S(1)} %get-tuple-element.130), channel_id=1, source_target_pairs={{0,8},{8,16},{16,24},{1,9},{9,17},{17,25},{2,10},{10,18},{18,26},{... | collective-permute-start | bytes 147464 | tf_op jit(solution)/shard_map/ppermute | solution.py:20
  120.1 22.2 %collective-permute-start.10 = (bf16[48,20,2]{2,0,1:T(8,128)(2,1)S(1)}, bf16[48,20,2]{2,0,1:T(8,128)(2,1)S(1)}, u32[]{:S(2)}, u32[]{:S(2)}) collective-permute-start(bf16[48,20,2]{2,0,1:T(8,128)(2,1)S(1)} %get-tuple-element.160), channel_id=1, source_target_pairs={{0,1},{1,2},{2,3},{3,4},{4,5},{5,6},{6,7},{8,9},{9,10},{10,11},{11... | collective-permute-start | bytes 11528 | tf_op jit(solution)/shard_map/ppermute | solution.py:20
  123.7 18.5 %collective-permute-start.11 = (bf16[48,20,2]{2,0,1:T(8,128)(2,1)S(1)}, bf16[48,20,2]{2,0,1:T(8,128)(2,1)S(1)}, u32[]{:S(2)}, u32[]{:S(2)}) collective-permute-start(bf16[48,20,2]{2,0,1:T(8,128)(2,1)S(1)} %get-tuple-element.161), channel_id=1, source_target_pairs={{1,0},{2,1},{3,2},{4,3},{5,4},{6,5},{7,6},{9,8},{10,9},{11,10},{12... | collective-permute-start | bytes 11528 | tf_op jit(solution)/shard_map/ppermute | solution.py:23
  142.0 373.5 %all-reduce.9.cloned.1.call-start = ((), (), s32[]{:S(2)}) async-start(), calls=%async_computation.1 | async-start | bytes 884736 | tf_op jit(solution)/shard_map/psum | solution.py:114
  154.3 120.0 %collective-permute-start.12 = (bf16[48,2,256]{0,1,2:T(2,128)(2,1)S(1)}, bf16[48,2,256]{0,1,2:T(2,128)(2,1)S(1)}, u32[]{:S(2)}, u32[]{:S(2)}) collective-permute-start(bf16[48,2,256]{0,1,2:T(2,128)(2,1)S(1)} %get-tuple-element.128), channel_id=1, source_target_pairs={{0,8},{8,16},{16,24},{1,9},{9,17},{17,25},{2,10},{10,18},{18,26},{... | collective-permute-start | bytes 147464 | tf_op jit(solution)/shard_map/ppermute | solution.py:20
  156.8 117.6 %collective-permute-start.13 = (bf16[48,2,256]{0,1,2:T(2,128)(2,1)S(1)}, bf16[48,2,256]{0,1,2:T(2,128)(2,1)S(1)}, u32[]{:S(2)}, u32[]{:S(2)}) collective-permute-start(bf16[48,2,256]{0,1,2:T(2,128)(2,1)S(1)} %get-tuple-element.129), channel_id=1, source_target_pairs={{8,0},{16,8},{24,16},{9,1},{17,9},{25,17},{10,2},{18,10},{26,18},{... | collective-permute-start | bytes 147464 | tf_op jit(solution)/shard_map/ppermute | solution.py:23
  274.7 12.3 %collective-permute-start.14 = (bf16[48,20,2]{2,0,1:T(8,128)(2,1)S(1)}, bf16[48,20,2]{2,0,1:T(8,128)(2,1)S(1)}, u32[]{:S(2)}, u32[]{:S(2)}) collective-permute-start(bf16[48,20,2]{2,0,1:T(8,128)(2,1)S(1)} %get-tuple-element.158), channel_id=1, source_target_pairs={{0,1},{1,2},{2,3},{3,4},{4,5},{5,6},{6,7},{8,9},{9,10},{10,11},{11... | collective-permute-start | bytes 11528 | tf_op jit(solution)/shard_map/ppermute | solution.py:20
  278.1 10.6 %collective-permute-start.15 = (bf16[48,20,2]{2,0,1:T(8,128)(2,1)S(1)}, bf16[48,20,2]{2,0,1:T(8,128)(2,1)S(1)}, u32[]{:S(2)}, u32[]{:S(2)}) collective-permute-start(bf16[48,20,2]{2,0,1:T(8,128)(2,1)S(1)} %get-tuple-element.159), channel_id=1, source_target_pairs={{1,0},{2,1},{3,2},{4,3},{5,4},{6,5},{7,6},{9,8},{10,9},{11,10},{12... | collective-permute-start | bytes 11528 | tf_op jit(solution)/shard_map/ppermute | solution.py:23
  335.6 13.3 %collective-permute-start.19 = (f32[48,16,1]{0,1,2:T(8,128)S(1)}, f32[48,16,1]{0,1,2:T(8,128)S(1)}, u32[]{:S(2)}, u32[]{:S(2)}) collective-permute-start(f32[48,16,1]{0,1,2:T(8,128)S(1)} %slice.394), channel_id=1, source_target_pairs={{1,0},{2,1},{3,2},{4,3},{5,4},{6,5},{7,6},{9,8},{10,9},{11,10},{12... | collective-permute-start | bytes 9224 | tf_op jit(solution)/shard_map/ppermute | solution.py:31
  350.6 13.9 %collective-permute-start.20 = (bf16[48,2,256]{0,1,2:T(2,128)(2,1)S(1)}, bf16[48,2,256]{0,1,2:T(2,128)(2,1)S(1)}, u32[]{:S(2)}, u32[]{:S(2)}) collective-permute-start(bf16[48,2,256]{0,1,2:T(2,128)(2,1)S(1)} %get-tuple-element.126), channel_id=1, source_target_pairs={{0,8},{8,16},{16,24},{1,9},{9,17},{17,25},{2,10},{10,18},{18,26},{... | collective-permute-start | bytes 147464 | tf_op jit(solution)/shard_map/ppermute | solution.py:20
  364.9 22.2 %collective-permute-start.22 = (bf16[48,20,2]{2,0,1:T(8,128)(2,1)S(1)}, bf16[48,20,2]{2,0,1:T(8,128)(2,1)S(1)}, u32[]{:S(2)}, u32[]{:S(2)}) collective-permute-start(bf16[48,20,2]{2,0,1:T(8,128)(2,1)S(1)} %get-tuple-element.156), channel_id=1, source_target_pairs={{0,1},{1,2},{2,3},{3,4},{4,5},{5,6},{6,7},{8,9},{9,10},{10,11},{11... | collective-permute-start | bytes 11528 | tf_op jit(solution)/shard_map/ppermute | solution.py:20
  368.5 18.5 %collective-permute-start.23 = (bf16[48,20,2]{2,0,1:T(8,128)(2,1)S(1)}, bf16[48,20,2]{2,0,1:T(8,128)(2,1)S(1)}, u32[]{:S(2)}, u32[]{:S(2)}) collective-permute-start(bf16[48,20,2]{2,0,1:T(8,128)(2,1)S(1)} %get-tuple-element.157), channel_id=1, source_target_pairs={{1,0},{2,1},{3,2},{4,3},{5,4},{6,5},{7,6},{9,8},{10,9},{11,10},{12... | collective-permute-start | bytes 11528 | tf_op jit(solution)/shard_map/ppermute | solution.py:23
  386.6 380.8 %all-reduce.7.cloned.1.call-start = ((), (), s32[]{:S(2)}) async-start(), calls=%async_computation | async-start | bytes 884736 | tf_op jit(solution)/shard_map/psum | solution.py:114
  399.6 119.2 %collective-permute-start.24 = (bf16[48,2,256]{0,1,2:T(2,128)(2,1)S(1)}, bf16[48,2,256]{0,1,2:T(2,128)(2,1)S(1)}, u32[]{:S(2)}, u32[]{:S(2)}) collective-permute-start(bf16[48,2,256]{0,1,2:T(2,128)(2,1)S(1)} %get-tuple-element.124), channel_id=1, source_target_pairs={{0,8},{8,16},{16,24},{1,9},{9,17},{17,25},{2,10},{10,18},{18,26},{... | collective-permute-start | bytes 147464 | tf_op jit(solution)/shard_map/ppermute | solution.py:20
  402.1 116.8 %collective-permute-start.25 = (bf16[48,2,256]{0,1,2:T(2,128)(2,1)S(1)}, bf16[48,2,256]{0,1,2:T(2,128)(2,1)S(1)}, u32[]{:S(2)}, u32[]{:S(2)}) collective-permute-start(bf16[48,2,256]{0,1,2:T(2,128)(2,1)S(1)} %get-tuple-element.125), channel_id=1, source_target_pairs={{8,0},{16,8},{24,16},{9,1},{17,9},{25,17},{10,2},{18,10},{26,18},{... | collective-permute-start | bytes 147464 | tf_op jit(solution)/shard_map/ppermute | solution.py:23
  519.3 12.3 %collective-permute-start.26 = (bf16[48,20,2]{2,0,1:T(8,128)(2,1)S(1)}, bf16[48,20,2]{2,0,1:T(8,128)(2,1)S(1)}, u32[]{:S(2)}, u32[]{:S(2)}) collective-permute-start(bf16[48,20,2]{2,0,1:T(8,128)(2,1)S(1)} %get-tuple-element.154), channel_id=1, source_target_pairs={{0,1},{1,2},{2,3},{3,4},{4,5},{5,6},{6,7},{8,9},{9,10},{10,11},{11... | collective-permute-start | bytes 11528 | tf_op jit(solution)/shard_map/ppermute | solution.py:20
  522.6 10.6 %collective-permute-start.27 = (bf16[48,20,2]{2,0,1:T(8,128)(2,1)S(1)}, bf16[48,20,2]{2,0,1:T(8,128)(2,1)S(1)}, u32[]{:S(2)}, u32[]{:S(2)}) collective-permute-start(bf16[48,20,2]{2,0,1:T(8,128)(2,1)S(1)} %get-tuple-element.155), channel_id=1, source_target_pairs={{1,0},{2,1},{3,2},{4,3},{5,4},{6,5},{7,6},{9,8},{10,9},{11,10},{12... | collective-permute-start | bytes 11528 | tf_op jit(solution)/shard_map/ppermute | solution.py:23
  573.2 14.4 %collective-permute-start.30 = (bf16[48,1,257]{0,1,2:T(2,128)(2,1)}, bf16[48,1,257]{0,1,2:T(2,128)(2,1)}, u32[]{:S(2)}, u32[]{:S(2)}) collective-permute-start(bf16[48,1,257]{0,1,2:T(2,128)(2,1)} %slice.527), channel_id=1, source_target_pairs={{8,0},{16,8},{24,16},{9,1},{17,9},{25,17},{10,2},{18,10},{26,18},{... | collective-permute-start | bytes 74024 | tf_op jit(solution)/shard_map/ppermute | solution.py:31
  594.8 9.2 %collective-permute-start.31 = (f32[48,16,1]{0,1,2:T(8,128)S(1)}, f32[48,16,1]{0,1,2:T(8,128)S(1)}, u32[]{:S(2)}, u32[]{:S(2)}) collective-permute-start(f32[48,16,1]{0,1,2:T(8,128)S(1)} %slice.419), channel_id=1, source_target_pairs={{1,0},{2,1},{3,2},{4,3},{5,4},{6,5},{7,6},{9,8},{10,9},{11,10},{12... | collective-permute-start | bytes 9224 | tf_op jit(solution)/shard_map/ppermute | solution.py:31
  615.3 21.8 %collective-permute-start.34 = (bf16[48,20,2]{2,0,1:T(8,128)(2,1)S(1)}, bf16[48,20,2]{2,0,1:T(8,128)(2,1)S(1)}, u32[]{:S(2)}, u32[]{:S(2)}) collective-permute-start(bf16[48,20,2]{2,0,1:T(8,128)(2,1)S(1)} %get-tuple-element.152), channel_id=1, source_target_pairs={{0,1},{1,2},{2,3},{3,4},{4,5},{5,6},{6,7},{8,9},{9,10},{10,11},{11... | collective-permute-start | bytes 11528 | tf_op jit(solution)/shard_map/ppermute | solution.py:20
  619.2 17.8 %collective-permute-start.35 = (bf16[48,20,2]{2,0,1:T(8,128)(2,1)S(1)}, bf16[48,20,2]{2,0,1:T(8,128)(2,1)S(1)}, u32[]{:S(2)}, u32[]{:S(2)}) collective-permute-start(bf16[48,20,2]{2,0,1:T(8,128)(2,1)S(1)} %get-tuple-element.153), channel_id=1, source_target_pairs={{1,0},{2,1},{3,2},{4,3},{5,4},{6,5},{7,6},{9,8},{10,9},{11,10},{12... | collective-permute-start | bytes 11528 | tf_op jit(solution)/shard_map/ppermute | solution.py:23
  (83 other events, 1533.5 us)
Sparse Core Ops, SparseCore 0:
  142.1 129.6 all-reduce.10
  386.7 128.7 all-reduce.8
  637.1 130.2 all-reduce.6
where the time goes:
time: 792 us; the launch traced here: 782 us
  waiting for transfers between devices  378 us (48%)
  local copies, waits for them, and re-layouts  163 us (21%)
  starting transfers between devices  95.5 us (12%)
  matrix products  89.8 us (11%)
  other arithmetic  35.4 us (4%)
  between operations  20.5 us (3%)
    psum x3, waiting for transfers between devices, body(): grad_one = lax.psum(grad_one, ('rows', 'cols'))  343 us
    transpose x6, matrix products, kernel_grad(): return jnp.transpose(summed, (1, 0, 2, 3))  62.4 us
    conv_general_dilated x33, local copies, waits for them, and re-layouts, plain_conv(): lax.conv_general_dilated(source[None], kernel, (stride, stride), 'VALID',...  54.5 us
    ppermute x12, starting transfers between devices, with_halo(): lax.ppermute(lax.slice_in_dim(block, block.shape[dim] - width, None, axis...  44.4 us
    broadcast_in_dim x15, local copies, waits for them, and re-layouts, plain_conv(): source[None]  32 us
    ppermute x12, starting transfers between devices, with_halo(): lax.ppermute(lax.slice_in_dim(block, 0, width, axis=dim), axis, backward)  27.7 us
    unnamed x149, local copies, waits for them, and re-layouts  26.4 us
    conv_general_dilated x9, matrix products, plain_conv(): lax.conv_general_dilated(source[None], kernel, (stride, stride), 'VALID',...  23.4 us
  transfers between devices with their start and end apart: 39, of which 16 were waited for; matrix products, arithmetic and copies ran while one was open for 20% of the time, Pallas kernels for 0%

commit v1 on v0

--- a/solution.py
+++ b/solution.py
@@ -10,6 +10,10 @@
 learn_rate = 0.005
 mean_epsilon = 1e-06
 numbers = ("NCHW", "OIHW", "NCHW")
+
+
+def rest_desk_now(view):
+    return lax.all_gather(view, ("rows", "cols")).sum(axis=0)
 
 
 def with_halo(block, sides, width):
@@ -111,7 +115,7 @@
         input_grad = plain_conv(grad_rimmed, flipped(fast_one), 1, 2)
         grad_one = kernel_grad(beside_all, pre_grad, 1, 2)
         perturb = jnp.clip(perturb + step_size * jnp.tanh(input_grad), -clip_bound, clip_bound)
-        grad_one = lax.psum(grad_one, ("rows", "cols"))
+        grad_one = rest_desk_now(grad_one)
         new_one, new_moment_one = normed_update(
             learned[0], learned[1], grad_one, jnp.mean(grad_one * grad_one)
         )

time: 792 us -> 921 us (1.16)
  waiting for transfers between devices: 378 us -> 483 us
  other arithmetic: 35.4 us -> 54.6 us
  local copies, waits for them, and re-layouts: 163 us -> 175 us
    all_gather x0 -> x3, waiting for transfers between devices: none -> 204 us  [rest_desk_now(): return lax.all_gather(view, ('rows', 'cols')).sum(axis=0)]
    psum x3, waiting for transfers between devices: 343 us -> 226 us  [body(): grad_two = lax.psum(grad_two, ('rows', 'cols'))]
    ppermute x12, waiting for transfers between devices: 13.2 us -> 32.4 us  [with_halo(): lax.ppermute(lax.slice_in_dim(block, 0, width, axis=dim), axis, backward)]
    reduce_sum x0 -> x3, other arithmetic: none -> 17.7 us  [rest_desk_now(): return lax.all_gather(view, ('rows', 'cols')).sum(axis=0)]
    unnamed x149 -> x155, local copies, waits for them, and re-layouts: 26.4 us -> 29.1 us
  transfers between devices with their start and end apart: 39 -> 42, of which waited for: 16 -> 21; matrix products, arithmetic and copies ran while one was open for 20% -> 20% of each run, Pallas kernels for 0% -> 0%
where the time goes in v1:
time: 921 us; the launch traced here: 910 us
  waiting for transfers between devices  483 us (52%)
  local copies, waits for them, and re-layouts  175 us (19%)
  starting transfers between devices  92.8 us (10%)
  matrix products  83.8 us (9%)
  other arithmetic  54.6 us (6%)
  between operations  20.8 us (2%)
    psum x3, waiting for transfers between devices, body(): grad_two = lax.psum(grad_two, ('rows', 'cols'))  226 us
    all_gather x3, waiting for transfers between devices, rest_desk_now(): return lax.all_gather(view, ('rows', 'cols')).sum(axis=0)  204 us
    transpose x6, matrix products, kernel_grad(): return jnp.transpose(summed, (1, 0, 2, 3))  57.8 us
    conv_general_dilated x33, local copies, waits for them, and re-layouts, plain_conv(): lax.conv_general_dilated(source[None], kernel, (stride, stride), 'VALID',...  54.3 us
    ppermute x12, starting transfers between devices, with_halo(): lax.ppermute(lax.slice_in_dim(block, block.shape[dim] - width, None, axis...  38.2 us
    ppermute x12, waiting for transfers between devices, with_halo(): lax.ppermute(lax.slice_in_dim(block, 0, width, axis=dim), axis, backward)  32.4 us
    broadcast_in_dim x15, local copies, waits for them, and re-layouts, plain_conv(): source[None]  32.1 us
    unnamed x155, local copies, waits for them, and re-layouts  29.1 us
  transfers between devices with their start and end apart: 42, of which 21 were waited for; matrix products, arithmetic and copies ran while one was open for 20% of the time, Pallas kernels for 0%

profile of v1, /device:TPU:8, one launch (start us, length us, event | category | flops | bytes accessed | tf_op | source)
XLA Modules:
  0.0 910.0 jit_solution(5821307801060761890)
XLA Ops:
  28.6 7.8 collective-permute-done.3
  79.6 5.0 copy.412
  94.1 5.1 scatter-add.20
  101.9 6.9 fusion.109
  113.5 12.3 %fusion.22 = f32[48,48,3,3]{0,1,3,2:T(8,128)S(1)} fusion(bf16[1,48,20,260]{1,0,3,2:T(2,128)(2,1)S(1)} %copy-done.24, bf16[1,48,16,256]{1,2,3,0:T(8,128)(2,1)S(1)} %bitcast.273), kind=kOutput, calls=%fused_computation.48 | convolution fusion | flops 169869312 | bytes 975360 | tf_op jit(solution)/shard_map/transpose | solution.py:60
  144.2 8.3 collective-permute-done.11
  176.6 62.5 %all-reduce.4.cloned.1.call-done = f32[48,48,3,3]{0,1,3,2:T(8,128)} async-done(((f32[48,48,3,3]{0,1,3,2:T(8,128)}), f32[48,48,3,3]{0,1,3,2:T(8,128)}) %all-reduce.4.cloned.1.call-update) | async-done | bytes 82960 | tf_op jit(solution)/shard_map/psum | solution.py:107
  248.6 74.6 %all-gather.7.cloned.1.call-done = f32[1536,48,3,3]{1,3,2,0:T(4,128)} async-done(((f32[48,48,3,3]{1,3,2,0:T(4,128)}), f32[1536,48,3,3]{1,3,2,0:T(4,128)}) %all-gather.7.cloned.1.call-update) | async-done | bytes 2654224 | tf_op jit(solution)/shard_map/all_gather | solution.py:16
  323.1 5.9 reduce_sum.81
  364.5 5.0 copy.442
  379.0 5.1 scatter-add.24
  387.3 6.9 fusion.107
  398.7 12.3 %fusion.20 = f32[48,48,3,3]{0,1,3,2:T(8,128)S(1)} fusion(bf16[1,48,20,260]{1,0,3,2:T(2,128)(2,1)S(1)} %copy-done.25, bf16[1,48,16,256]{1,2,3,0:T(8,128)(2,1)S(1)} %bitcast.274), kind=kOutput, calls=%fused_computation.46 | convolution fusion | flops 169869312 | bytes 975360 | tf_op jit(solution)/shard_map/transpose | solution.py:60
  430.4 8.0 collective-permute-done.23
  463.3 61.2 %all-reduce.6.cloned.1.call-done = f32[48,48,3,3]{0,1,3,2:T(8,128)} async-done(((f32[48,48,3,3]{0,1,3,2:T(8,128)}), f32[48,48,3,3]{0,1,3,2:T(8,128)}) %all-reduce.6.cloned.1.call-update) | async-done | bytes 82960 | tf_op jit(solution)/shard_map/psum | solution.py:107
  533.0 75.4 %all-gather.9.cloned.1.call-done = f32[1536,48,3,3]{1,3,2,0:T(4,128)} async-done(((f32[48,48,3,3]{1,3,2,0:T(4,128)}), f32[1536,48,3,3]{1,3,2,0:T(4,128)}) %all-gather.9.cloned.1.call-update) | async-done | bytes 2654224 | tf_op jit(solution)/shard_map/all_gather | solution.py:16
  608.4 5.9 reduce_sum.84
  664.2 5.1 scatter-add.26
  672.4 6.9 fusion.105
  683.9 12.3 %fusion.18 = f32[48,48,3,3]{0,1,3,2:T(8,128)S(1)} fusion(bf16[1,48,20,260]{1,0,3,2:T(2,128)(2,1)S(1)} %copy-done.23, bf16[1,48,16,256]{1,2,3,0:T(8,128)(2,1)S(1)} %bitcast.275), kind=kOutput, calls=%fused_computation.44 | convolution fusion | flops 169869312 | bytes 975360 | tf_op jit(solution)/shard_map/transpose | solution.py:60
  705.7 102.3 %all-reduce.8.cloned.1.call-done = f32[48,48,3,3]{0,1,3,2:T(8,128)} async-done(((f32[48,48,3,3]{0,1,3,2:T(8,128)}), f32[48,48,3,3]{0,1,3,2:T(8,128)}) %all-reduce.8.cloned.1.call-update) | async-done | bytes 82960 | tf_op jit(solution)/shard_map/psum | solution.py:107
  819.3 5.9 collective-permute-done.34
  839.5 53.9 %all-gather.11.cloned.1.call-done = f32[1536,48,3,3]{1,3,2,0:T(4,128)} async-done(((f32[48,48,3,3]{1,3,2,0:T(4,128)}), f32[1536,48,3,3]{1,3,2,0:T(4,128)}) %all-gather.11.cloned.1.call-update) | async-done | bytes 2654224 | tf_op jit(solution)/shard_map/all_gather | solution.py:16
  893.5 5.9 reduce_sum.87
  (421 shorter events, 328.6 us)
Async XLA Ops:
  7.2 231.9 %all-reduce.4.cloned.1.call-start = ((), (), s32[]{:S(2)}) async-start(), calls=%async_computation | async-start | bytes 442368 | tf_op jit(solution)/shard_map/psum | solution.py:107
  19.6 9.0 collective-permute-start.2
  23.0 13.4 %collective-permute-start.3 = (bf16[48,20,2]{2,0,1:T(8,128)(2,1)S(1)}, bf16[48,20,2]{2,0,1:T(8,128)(2,1)S(1)}, u32[]{:S(2)}, u32[]{:S(2)}) collective-permute-start(bf16[48,20,2]{2,0,1:T(8,128)(2,1)S(1)} %get-tuple-element.163), channel_id=1, source_target_pairs={{1,0},{2,1},{3,2},{4,3},{5,4},{6,5},{7,6},{9,8},{10,9},{11,10},{12... | collective-permute-start | bytes 11528 | tf_op jit(solution)/shard_map/ppermute | solution.py:27
  78.3 14.4 %collective-permute-start.6 = (bf16[48,1,257]{0,1,2:T(2,128)(2,1)S(1)}, bf16[48,1,257]{0,1,2:T(2,128)(2,1)S(1)}, u32[]{:S(2)}, u32[]{:S(2)}) collective-permute-start(bf16[48,1,257]{0,1,2:T(2,128)(2,1)S(1)} %slice.529), channel_id=1, source_target_pairs={{8,0},{16,8},{24,16},{9,1},{17,9},{25,17},{10,2},{18,10},{26,18},{... | collective-permute-start | bytes 74024 | tf_op jit(solution)/shard_map/ppermute | solution.py:35
  99.9 11.1 %collective-permute-start.7 = (f32[48,16,1]{0,1,2:T(8,128)S(1)}, f32[48,16,1]{0,1,2:T(8,128)S(1)}, u32[]{:S(2)}, u32[]{:S(2)}) collective-permute-start(f32[48,16,1]{0,1,2:T(8,128)S(1)} %slice.369), channel_id=1, source_target_pairs={{1,0},{2,1},{3,2},{4,3},{5,4},{6,5},{7,6},{9,8},{10,9},{11,10},{12... | collective-permute-start | bytes 9224 | tf_op jit(solution)/shard_map/ppermute | solution.py:35
  108.9 214.2 %all-gather.7.cloned.1.call-start = ((), (), s32[]{:S(2)}) async-start(), calls=%async_computation.3 | async-start | bytes 9732096 | tf_op jit(solution)/shard_map/all_gather | solution.py:16
  126.7 397.8 %all-reduce.6.cloned.1.call-start = ((), (), s32[]{:S(2)}) async-start(), calls=%async_computation.1 | async-start | bytes 442368 | tf_op jit(solution)/shard_map/psum | solution.py:107
  139.1 13.3 %collective-permute-start.11 = (bf16[48,20,2]{2,0,1:T(8,128)(2,1)S(1)}, bf16[48,20,2]{2,0,1:T(8,128)(2,1)S(1)}, u32[]{:S(2)}, u32[]{:S(2)}) collective-permute-start(bf16[48,20,2]{2,0,1:T(8,128)(2,1)S(1)} %get-tuple-element.161), channel_id=1, source_target_pairs={{1,0},{2,1},{3,2},{4,3},{5,4},{6,5},{7,6},{9,8},{10,9},{11,10},{12... | collective-permute-start | bytes 11528 | tf_op jit(solution)/shard_map/ppermute | solution.py:27
  169.7 71.7 %collective-permute-start.14 = (bf16[48,20,2]{2,0,1:T(8,128)(2,1)S(1)}, bf16[48,20,2]{2,0,1:T(8,128)(2,1)S(1)}, u32[]{:S(2)}, u32[]{:S(2)}) collective-permute-start(bf16[48,20,2]{2,0,1:T(8,128)(2,1)S(1)} %get-tuple-element.158), channel_id=1, source_target_pairs={{0,1},{1,2},{2,3},{3,4},{4,5},{5,6},{6,7},{8,9},{9,10},{10,11},{11... | collective-permute-start | bytes 11528 | tf_op jit(solution)/shard_map/ppermute | solution.py:24
  172.6 68.8 %collective-permute-start.15 = (bf16[48,20,2]{2,0,1:T(8,128)(2,1)S(1)}, bf16[48,20,2]{2,0,1:T(8,128)(2,1)S(1)}, u32[]{:S(2)}, u32[]{:S(2)}) collective-permute-start(bf16[48,20,2]{2,0,1:T(8,128)(2,1)S(1)} %get-tuple-element.159), channel_id=1, source_target_pairs={{1,0},{2,1},{3,2},{4,3},{5,4},{6,5},{7,6},{9,8},{10,9},{11,10},{12... | collective-permute-start | bytes 11528 | tf_op jit(solution)/shard_map/ppermute | solution.py:27
  363.2 14.4 %collective-permute-start.18 = (bf16[48,1,257]{0,1,2:T(2,128)(2,1)}, bf16[48,1,257]{0,1,2:T(2,128)(2,1)}, u32[]{:S(2)}, u32[]{:S(2)}) collective-permute-start(bf16[48,1,257]{0,1,2:T(2,128)(2,1)} %slice.528), channel_id=1, source_target_pairs={{8,0},{16,8},{24,16},{9,1},{17,9},{25,17},{10,2},{18,10},{26,18},{... | collective-permute-start | bytes 74024 | tf_op jit(solution)/shard_map/ppermute | solution.py:35
  384.8 11.4 %collective-permute-start.19 = (f32[48,16,1]{0,1,2:T(8,128)S(1)}, f32[48,16,1]{0,1,2:T(8,128)S(1)}, u32[]{:S(2)}, u32[]{:S(2)}) collective-permute-start(f32[48,16,1]{0,1,2:T(8,128)S(1)} %slice.394), channel_id=1, source_target_pairs={{1,0},{2,1},{3,2},{4,3},{5,4},{6,5},{7,6},{9,8},{10,9},{11,10},{12... | collective-permute-start | bytes 9224 | tf_op jit(solution)/shard_map/ppermute | solution.py:35
  394.2 214.2 %all-gather.9.cloned.1.call-start = ((), (), s32[]{:S(2)}) async-start(), calls=%async_computation.4 | async-start | bytes 9732096 | tf_op jit(solution)/shard_map/all_gather | solution.py:16
  411.8 396.2 %all-reduce.8.cloned.1.call-start = ((), (), s32[]{:S(2)}) async-start(), calls=%async_computation.2 | async-start | bytes 442368 | tf_op jit(solution)/shard_map/psum | solution.py:107
  425.4 13.1 %collective-permute-start.23 = (bf16[48,20,2]{2,0,1:T(8,128)(2,1)S(1)}, bf16[48,20,2]{2,0,1:T(8,128)(2,1)S(1)}, u32[]{:S(2)}, u32[]{:S(2)}) collective-permute-start(bf16[48,20,2]{2,0,1:T(8,128)(2,1)S(1)} %get-tuple-element.157), channel_id=1, source_target_pairs={{1,0},{2,1},{3,2},{4,3},{5,4},{6,5},{7,6},{9,8},{10,9},{11,10},{12... | collective-permute-start | bytes 11528 | tf_op jit(solution)/shard_map/ppermute | solution.py:27
  456.2 70.7 %collective-permute-start.26 = (bf16[48,20,2]{2,0,1:T(8,128)(2,1)S(1)}, bf16[48,20,2]{2,0,1:T(8,128)(2,1)S(1)}, u32[]{:S(2)}, u32[]{:S(2)}) collective-permute-start(bf16[48,20,2]{2,0,1:T(8,128)(2,1)S(1)} %get-tuple-element.154), channel_id=1, source_target_pairs={{0,1},{1,2},{2,3},{3,4},{4,5},{5,6},{6,7},{8,9},{9,10},{10,11},{11... | collective-permute-start | bytes 11528 | tf_op jit(solution)/shard_map/ppermute | solution.py:24
  459.0 67.9 %collective-permute-start.27 = (bf16[48,20,2]{2,0,1:T(8,128)(2,1)S(1)}, bf16[48,20,2]{2,0,1:T(8,128)(2,1)S(1)}, u32[]{:S(2)}, u32[]{:S(2)}) collective-permute-start(bf16[48,20,2]{2,0,1:T(8,128)(2,1)S(1)} %get-tuple-element.155), channel_id=1, source_target_pairs={{1,0},{2,1},{3,2},{4,3},{5,4},{6,5},{7,6},{9,8},{10,9},{11,10},{12... | collective-permute-start | bytes 11528 | tf_op jit(solution)/shard_map/ppermute | solution.py:27
  648.4 14.4 %collective-permute-start.30 = (bf16[48,1,257]{0,1,2:T(2,128)(2,1)}, bf16[48,1,257]{0,1,2:T(2,128)(2,1)}, u32[]{:S(2)}, u32[]{:S(2)}) collective-permute-start(bf16[48,1,257]{0,1,2:T(2,128)(2,1)} %slice.527), channel_id=1, source_target_pairs={{8,0},{16,8},{24,16},{9,1},{17,9},{25,17},{10,2},{18,10},{26,18},{... | collective-permute-start | bytes 74024 | tf_op jit(solution)/shard_map/ppermute | solution.py:35
  670.0 11.5 %collective-permute-start.31 = (f32[48,16,1]{0,1,2:T(8,128)S(1)}, f32[48,16,1]{0,1,2:T(8,128)S(1)}, u32[]{:S(2)}, u32[]{:S(2)}) collective-permute-start(f32[48,16,1]{0,1,2:T(8,128)S(1)} %slice.419), channel_id=1, source_target_pairs={{1,0},{2,1},{3,2},{4,3},{5,4},{6,5},{7,6},{9,8},{10,9},{11,10},{12... | collective-permute-start | bytes 9224 | tf_op jit(solution)/shard_map/ppermute | solution.py:35
  679.4 214.1 %all-gather.11.cloned.1.call-start = ((), (), s32[]{:S(2)}) async-start(), calls=%async_computation.5 | async-start | bytes 9732096 | tf_op jit(solution)/shard_map/all_gather | solution.py:16
  700.3 110.1 %collective-permute-start.32 = (bf16[48,2,256]{0,1,2:T(2,128)(2,1)S(1)}, bf16[48,2,256]{0,1,2:T(2,128)(2,1)S(1)}, u32[]{:S(2)}, u32[]{:S(2)}) collective-permute-start(bf16[48,2,256]{0,1,2:T(2,128)(2,1)S(1)} %get-tuple-element.122), channel_id=1, source_target_pairs={{0,8},{8,16},{16,24},{1,9},{9,17},{17,25},{2,10},{10,18},{18,26},{... | collective-permute-start | bytes 147464 | tf_op jit(solution)/shard_map/ppermute | solution.py:24
  704.4 106.1 %collective-permute-start.33 = (bf16[48,2,256]{0,1,2:T(2,128)(2,1)S(1)}, bf16[48,2,256]{0,1,2:T(2,128)(2,1)S(1)}, u32[]{:S(2)}, u32[]{:S(2)}) collective-permute-start(bf16[48,2,256]{0,1,2:T(2,128)(2,1)S(1)} %get-tuple-element.123), channel_id=1, source_target_pairs={{8,0},{16,8},{24,16},{9,1},{17,9},{25,17},{10,2},{18,10},{26,18},{... | collective-permute-start | bytes 147464 | tf_op jit(solution)/shard_map/ppermute | solution.py:27
  810.8 14.4 %collective-permute-start.34 = (bf16[48,20,2]{2,0,1:T(8,128)(2,1)S(1)}, bf16[48,20,2]{2,0,1:T(8,128)(2,1)S(1)}, u32[]{:S(2)}, u32[]{:S(2)}) collective-permute-start(bf16[48,20,2]{2,0,1:T(8,128)(2,1)S(1)} %get-tuple-element.152), channel_id=1, source_target_pairs={{0,1},{1,2},{2,3},{3,4},{4,5},{5,6},{6,7},{8,9},{9,10},{10,11},{11... | collective-permute-start | bytes 11528 | tf_op jit(solution)/shard_map/ppermute | solution.py:24
  814.2 12.5 %collective-permute-start.35 = (bf16[48,20,2]{2,0,1:T(8,128)(2,1)S(1)}, bf16[48,20,2]{2,0,1:T(8,128)(2,1)S(1)}, u32[]{:S(2)}, u32[]{:S(2)}) collective-permute-start(bf16[48,20,2]{2,0,1:T(8,128)(2,1)S(1)} %get-tuple-element.153), channel_id=1, source_target_pairs={{1,0},{2,1},{3,2},{4,3},{5,4},{6,5},{7,6},{9,8},{10,9},{11,10},{12... | collective-permute-start | bytes 11528 | tf_op jit(solution)/shard_map/ppermute | solution.py:27
  (89 other events, 1082.4 us)
Sparse Core Ops, SparseCore 0:
  109.0 130.0 all-reduce.3
  242.0 81.0 all-gather.6
  394.4 130.1 all-reduce.5
  527.3 81.0 all-gather.8
  679.5 128.4 all-reduce.7
  810.8 82.6 all-gather.10
